TPU v7x, 128 devices: a whole 4x4x4 slice. The times are simulated.
128 devices in a mesh: dp: 8 (over x_lo, z), cell: 16 (over x_hi, y, core).
Axes of the slice: x: 4 (x_hi: 2, x_lo: 2; x = x_hi * 2 + x_lo), y: 4, z: 4, core: 2. Of those that a mesh axis runs over, the one named last changes fastest.
Arguments:
- sensitivity: float32 [4096, 65536], P(('dp', 'cell')), may hold values from -0.09375 to 0.09375
- row_period: int32 [4096], P(('dp', 'cell')), may hold values from 0 to 31
- row_site: int32 [4096], P(('dp', 'cell')), may hold values from 0 to 127
- period_err: float32 [32], replicated, may hold values from 0.2 to 2
- site_err: float32 [128], replicated, may hold values from 0.2 to 2
- cell_var: float32 [65536], replicated, may hold values from 0.25 to 4
- cell_perm: int32 [65536], replicated, may hold values from 0 to 65535, each once
Outputs:
- gram: float32 [4096, 4096], P('cell', 'dp')
Inputs may be any that keep to these rules, and one draw needn't show every extreme that they name: `cell_perm`: a permutation of 0 to 65535.
All inputs are finite; a program needn't handle non-finite values.
Results may differ from a plain program's by a relative error of at most 0.0009.
Values may be sent and summed in bfloat16 or wider, within the bound.
No kernel may reach another device: no remote copies, remote signals or barrier semaphores. Data moves between devices by JAX's collectives and lax.ppermute only.
A program may use at most 128 MiB of HBM per device.

v0:
```python
import jax
import jax.numpy as jnp
from jax import lax
from jax.sharding import PartitionSpec as P


def pack_rows(sensitivity, row_period, row_site, period_err, site_err):
    period_hit = row_period[:, None] == jnp.arange(period_err.shape[0], dtype=jnp.int32)[None, :]
    site_hit = row_site[:, None] == jnp.arange(site_err.shape[0], dtype=jnp.int32)[None, :]
    period_scale = jnp.sum(jnp.where(period_hit, period_err[None, :], 0.0), axis=1)
    site_scale = jnp.sum(jnp.where(site_hit, site_err[None, :], 0.0), axis=1)
    row_weight = 1.0 / jnp.sqrt(period_scale * period_scale + site_scale * site_scale)
    return (row_weight[:, None] * sensitivity).astype(jnp.bfloat16)


def weigh_columns(scaled, cell_var, cell_perm, first_cell):
    width = scaled.shape[1]
    positions = lax.dynamic_slice_in_dim(cell_perm, first_cell, width)
    column_var = cell_var[positions]
    return (scaled.astype(jnp.float32) * column_var[None, :]).astype(jnp.bfloat16)


def against(rows_block, weighted):
    return lax.dot_general(
        rows_block, weighted, (((1,), (1,)), ((), ())), preferred_element_type=jnp.float32
    )


def body(sensitivity, row_period, row_site, period_err, site_err, cell_var, cell_perm):
    packed = pack_rows(sensitivity, row_period, row_site, period_err, site_err)
    total_cells = cell_var.shape[0]
    scaled = lax.all_to_all(packed, "cell", split_axis=1, concat_axis=0, tiled=True)
    first_cell = lax.axis_index("cell") * (total_cells // lax.axis_size("cell"))
    weighted = weigh_columns(scaled, cell_var, cell_perm, first_cell)
    partial_value = against(lax.all_gather(scaled, "dp", axis=0, tiled=True), weighted)
    gram = lax.psum_scatter(partial_value, "cell", scatter_dimension=0, tiled=True)
    return gram


def solution(mesh):
    return jax.shard_map(
        body,
        mesh=mesh,
        in_specs=(
            P(("dp", "cell"), None),
            P(("dp", "cell")),
            P(("dp", "cell")),
            P(),
            P(),
            P(),
            P(),
        ),
        out_specs=P("cell", "dp"),
        check_vma=False,
    )
```

profile of v0, /device:TPU:0, one launch (start us, length us, event | category | flops | bytes accessed | tf_op | source)
XLA Modules:
  0.0 530.3 jit_solution(9039433479260723975)
XLA Ops:
  6.5 0.0 copy-start
  6.5 0.0 all-gather.2.cloned.1.call-start
  6.5 0.9 select_reduce_fusion.1
  7.4 0.9 select_reduce_fusion
  8.3 3.9 multiply_convert_fusion.1
  12.2 0.3 copy.13
  12.5 58.7 %all_to_all.19 = bf16[32,16,4096]{2,0,1:T(8,128)(2,1)} all-to-all(bf16[32,16,4096]{2,0,1:T(8,128)(2,1)S(1)} %bitcast.11), channel_id=1, replica_groups=mesh['dp'=8,'cell'=16] {'cell'}, dimensions={1} | all-to-all | bytes 8388608 | tf_op jit(solution)/shard_map/all_to_all | solution.py:32
  71.2 0.0 all-gather.2.cloned.1.call-update
  71.2 0.0 reduce-scatter.2.cloned.1.call-start
  71.3 0.7 fusion.2
  72.0 0.0 copy-done
  72.0 23.0 %gather_fusion = f32[4096]{0:T(1024)S(1)} fusion(f32[65536]{0:T(1024)S(1)} %copy-done, s32[4096]{0:T(1024)S(1)} %fusion.2), kind=kCustom, calls=%fused_computation | custom fusion | bytes 49152 | tf_op jit(solution)/shard_map/gather | solution.py:19
  95.1 302.5 %all-gather.2.cloned.1.call-done = bf16[4096,4096]{1,0:T(8,128)(2,1)} async-done(((bf16[512,4096]{1,0:T(8,128)(2,1)}), bf16[4096,4096]{1,0:T(8,128)(2,1)}) %all-gather.2.cloned.1.call-update) | async-done | bytes 33554448 | tf_op jit(solution)/shard_map/all_gather | solution.py:35
  397.5 25.0 %fusion = f32[4096,512]{1,0:T(8,128)} fusion(bf16[4096,4096]{1,0:T(8,128)(2,1)} %all-gather.2.cloned.1.call-done, bf16[512,4096]{1,0:T(8,128)(2,1)} %bitcast.9, f32[4096]{0:T(1024)S(1)} %gather_fusion), kind=kOutput, calls=%fused_computation.3 | convolution fusion | flops 17186160640 | bytes 46153728 | tf_op jit(solution)/shard_map/dot_general | solution.py:24
  422.5 0.0 reduce-scatter.2.cloned.1.call-update
  422.5 101.0 %reduce-scatter.2.cloned.1.call-done = f32[256,512]{1,0:T(8,128)} async-done(((f32[4096,512]{1,0:T(8,128)}), f32[256,512]{1,0:T(8,128)}) %reduce-scatter.2.cloned.1.call-update) | async-done | bytes 524304 | tf_op jit(solution)/shard_map/reduce_scatter | solution.py:36
  (1 shorter events, 0.0 us)
Async XLA Ops:
  6.5 65.5 %copy-start = (f32[65536]{0:T(1024)S(1)}, f32[65536]{0:T(1024)}, u32[]{:S(2)}) copy-start(f32[65536]{0:T(1024)} %param.12) | copy-start | bytes 786436
  6.5 391.0 %all-gather.2.cloned.1.call-start = ((), (), s32[]{:S(2)}) async-start(), calls=%async_computation.2 | async-start | bytes 37748736 | tf_op jit(solution)/shard_map/all_gather | solution.py:35
  71.2 452.3 %reduce-scatter.2.cloned.1.call-start = ((), (), s32[]{:S(2)}) async-start(), calls=%async_computation.3 | async-start | bytes 8912896 | tf_op jit(solution)/shard_map/reduce_scatter | solution.py:36
Sparse Core Ops, SparseCore 0:
  71.4 326.1 all-gather.1
  422.7 100.7 reduce-scatter.1
where the time goes:
time: 531 us; the launch traced here: 530 us
  waiting for transfers between devices  403 us (76%)
  blocking collectives  58.7 us (11%)
  matrix products  25 us (5%)
  local copies, waits for them, and re-layouts  23.3 us (4%)
  between operations  13.4 us (3%)
  other arithmetic  6.41 us (1%)
    all_gather x1, waiting for transfers between devices, body(): lax.all_gather(scaled, 'dp', axis=0, tiled=True)  302 us
    reduce_scatter x1, waiting for transfers between devices, body(): lax.psum_scatter(partial_value, 'cell', scatter_dimension=0, tiled=True)  101 us
    all_to_all x1, blocking collectives, body(): lax.all_to_all(packed, 'cell', split_axis=1, concat_axis=0, tiled=True)  58.7 us
    dot_general x1, matrix products, against(): lax.dot_general(rows_block, weighted, (((1,), (1,)), ((), ())), preferred...  25 us
    gather x1, local copies, waits for them, and re-layouts, weigh_columns(): column_var = cell_var[positions]  23 us
  transfers between devices with their start and end apart: 2, of which 2 were waited for; matrix products, arithmetic and copies ran while one was open for 4% of the time, Pallas kernels for 0%

commit v1 on v0

--- a/solution.py
+++ b/solution.py
@@ -32,7 +32,12 @@
     scaled = lax.all_to_all(packed, "cell", split_axis=1, concat_axis=0, tiled=True)
     first_cell = lax.axis_index("cell") * (total_cells // lax.axis_size("cell"))
     weighted = weigh_columns(scaled, cell_var, cell_perm, first_cell)
-    partial_value = against(lax.all_gather(scaled, "dp", axis=0, tiled=True), weighted)
+    partial_value = against(
+        jnp.concatenate(
+            lax.all_to_all(jnp.stack([scaled] * lax.axis_size("dp")), "dp", 0, 0), axis=0
+        ),
+        weighted,
+    )
     gram = lax.psum_scatter(partial_value, "cell", scatter_dimension=0, tiled=True)
     return gram
 

time: 531 us -> 586 us (1.10)
  waiting for transfers between devices: 403 us -> 433 us
  local copies, waits for them, and re-layouts: 23.3 us -> 36.2 us
  starting transfers between devices: 0.04 us -> 7.1 us
    all_to_all x0 -> x1, waiting for transfers between devices: none -> 335 us  [body(): lax.all_to_all(jnp.stack([scaled] * lax.axis_size('dp')), 'dp', 0, 0)]
    all_gather x1 -> x0, waiting for transfers between devices: 302 us -> none  [body(): lax.all_gather(scaled, 'dp', axis=0, tiled=True)]
    another operation x0 -> x1, local copies, waits for them, and re-layouts: none -> 10.9 us  [body(): jnp.stack([scaled] * lax.axis_size('dp'))]
    all_to_all x0 -> x1, starting transfers between devices: none -> 7.06 us  [body(): lax.all_to_all(jnp.stack([scaled] * lax.axis_size('dp')), 'dp', 0, 0)]
  transfers between devices with their start and end apart: 2 -> 2, of which waited for: 2 -> 2; matrix products, arithmetic and copies ran while one was open for 4% -> 5% of each run, Pallas kernels for 0% -> 0%
where the time goes in v1:
time: 586 us; the launch traced here: 585 us
  waiting for transfers between devices  433 us (74%)
  blocking collectives  58.6 us (10%)
  local copies, waits for them, and re-layouts  36.2 us (6%)
  matrix products  25 us (4%)
  between operations  13.4 us (2%)
  other arithmetic  11.7 us (2%)
  starting transfers between devices  7.1 us (1%)
    all_to_all x1, waiting for transfers between devices, body(): lax.all_to_all(jnp.stack([scaled] * lax.axis_size('dp')), 'dp', 0, 0)  335 us
    reduce_scatter x1, waiting for transfers between devices, body(): lax.psum_scatter(partial_value, 'cell', scatter_dimension=0, tiled=True)  98.7 us
    all_to_all x1, blocking collectives, body(): lax.all_to_all(packed, 'cell', split_axis=1, concat_axis=0, tiled=True)  58.6 us
    dot_general x1, matrix products, against(): lax.dot_general(rows_block, weighted, (((1,), (1,)), ((), ())), preferred...  25 us
    gather x1, local copies, waits for them, and re-layouts, weigh_columns(): column_var = cell_var[positions]  23 us
  transfers between devices with their start and end apart: 2, of which 2 were waited for; matrix products, arithmetic and copies ran while one was open for 5% of the time, Pallas kernels for 0%

profile of v1, /device:TPU:0, one launch (start us, length us, event | category | flops | bytes accessed | tf_op | source)
XLA Modules:
  0.0 585.4 jit_solution(14647596916848780406)
XLA Ops:
  6.5 0.0 copy-start
  6.5 0.9 select_reduce_fusion.1
  7.4 0.9 select_reduce_fusion
  8.3 3.9 multiply_convert_fusion.1
  12.2 0.3 copy.14
  12.5 58.6 %all_to_all.21 = bf16[32,16,4096]{2,0,1:T(8,128)(2,1)S(1)} all-to-all(bf16[32,16,4096]{2,0,1:T(8,128)(2,1)S(1)} %bitcast.14), channel_id=1, replica_groups=mesh['dp'=8,'cell'=16] {'cell'}, dimensions={1} | all-to-all | bytes 8388608 | tf_op jit(solution)/shard_map/all_to_all | solution.py:32
  71.1 0.0 copy-start.2
  71.1 1.9 copy-done.2
  73.0 10.9 %stack.5 = bf16[8,512,4096]{2,1,0:T(8,128)(2,1)} broadcast(bf16[512,4096]{1,0:T(8,128)(2,1)S(1)} %bitcast.12), dimensions={1,2} | broadcast | bytes 37748736 | tf_op jit(solution)/shard_map/stack | solution.py:37
  84.0 7.1 %all-to-all-start.1 = ((bf16[8,512,4096]{2,1,0:T(8,128)(2,1)}), bf16[8,512,4096]{2,1,0:T(8,128)(2,1)}, u32[]{:S(2)}, u32[]{:S(2)}) async-start(bf16[8,512,4096]{2,1,0:T(8,128)(2,1)} %stack.5), calls=%async_computation.1 | async-start | bytes 67108864 | tf_op jit(solution)/shard_map/all_to_all | solution.py:37
  91.0 0.0 reduce-scatter.2.cloned.1.call-start
  91.1 0.7 fusion
  91.8 0.0 copy-done
  91.8 23.0 %gather_fusion = f32[4096]{0:T(1024)S(1)} fusion(f32[65536]{0:T(1024)S(1)} %copy-done, s32[4096]{0:T(1024)S(1)} %fusion), kind=kCustom, calls=%fused_computation | custom fusion | bytes 49152 | tf_op jit(solution)/shard_map/gather | solution.py:19
  114.9 5.3 multiply_convert_fusion
  120.1 334.7 %all-to-all-done.1 = bf16[8,512,4096]{2,1,0:T(8,128)(2,1)} async-done(((bf16[8,512,4096]{2,1,0:T(8,128)(2,1)}), bf16[8,512,4096]{2,1,0:T(8,128)(2,1)}, u32[]{:S(2)}, u32[]{:S(2)}) %all-to-all-start.1) | async-done | bytes 33554464 | tf_op jit(solution)/shard_map/all_to_all | solution.py:37
  454.8 0.0 copy-start.1
  454.8 25.0 %fusion.1 = f32[4096,512]{1,0:T(8,128)} fusion(bf16[4096,4096]{1,0:T(8,128)(2,1)} %bitcast.2, bf16[512,4096]{1,0:T(8,128)(2,1)} %bitcast.15), kind=kOutput, calls=%fused_computation.11 | convolution fusion | flops 17179869184 | bytes 46137344 | tf_op jit(solution)/shard_map/dot_general | solution.py:24
  479.8 0.0 reduce-scatter.2.cloned.1.call-update
  479.9 98.7 %reduce-scatter.2.cloned.1.call-done = f32[256,512]{1,0:T(8,128)} async-done(((f32[4096,512]{1,0:T(8,128)}), f32[256,512]{1,0:T(8,128)}) %reduce-scatter.2.cloned.1.call-update) | async-done | bytes 524304 | tf_op jit(solution)/shard_map/reduce_scatter | solution.py:41
  578.6 0.0 copy-done.1
  (1 shorter events, 0.0 us)
Async XLA Ops:
  6.5 85.3 %copy-start = (f32[65536]{0:T(1024)S(1)}, f32[65536]{0:T(1024)}, u32[]{:S(2)}) copy-start(f32[65536]{0:T(1024)} %param.12) | copy-start | bytes 786436
  71.1 1.9 copy-start.2
  84.0 370.8 %all-to-all-start.1 = ((bf16[8,512,4096]{2,1,0:T(8,128)(2,1)}), bf16[8,512,4096]{2,1,0:T(8,128)(2,1)}, u32[]{:S(2)}, u32[]{:S(2)}) async-start(bf16[8,512,4096]{2,1,0:T(8,128)(2,1)} %stack.5), calls=%async_computation.1 | async-start | bytes 67108864 | tf_op jit(solution)/shard_map/all_to_all | solution.py:37
  91.0 487.5 %reduce-scatter.2.cloned.1.call-start = ((), (), s32[]{:S(2)}) async-start(), calls=%async_computation.3 | async-start | bytes 8912896 | tf_op jit(solution)/shard_map/reduce_scatter | solution.py:41
  454.8 123.8 %copy-start.1 = (f32[65536]{0:T(1024)S(1)}, f32[65536]{0:T(1024)}, u32[]{:S(2)}) copy-start(f32[65536]{0:T(1024)} %param.12) | copy-start | bytes 786436
Sparse Core Ops, SparseCore 0:
  480.0 98.5 reduce-scatter.1
